TPU v7x, 256 devices: a whole 4x4x8 slice. The times are simulated.
256 devices in a mesh: tok: 32 (over y, z), voc: 8 (over x, core).
Axes of the slice: x: 4, y: 4, z: 8, core: 2. Of those that a mesh axis runs over, the one named last changes fastest.
Arguments:
- teacher_rows: bfloat16 [8192, 2048], P('tok', 'voc')
- drafter_rows: bfloat16 [8192, 2048], P('tok', 'voc')
- head: bfloat16 [2048, 16384], P(None, 'voc'), may hold values from -1 to 1
- fr_ids: int32 [16384], P('voc'), may hold values from 0 to 151935, as said below
- targets: int32 [8192], P('tok'), may hold values from 0 to 151935
- dest_index: int32 [8192], P('tok'), may hold values from -1 to 8191, as said below
- counts: int32 [32], replicated, may hold values from 64 to 256, as said below
Outputs:
- row_loss: float32 [8192], P('tok')
- drafter_grad: bfloat16 [8192, 2048], P('tok', 'voc')
Inputs may be any that keep to these rules, and one draw needn't show every extreme that they name: `dest_index`: the prefill rows that name a slot name distinct slots. With blocks of 256 rows and 32 blocks, a row of prefill block b names a slot of drafter block (b + k) mod 32 for k in 0, 1, 16, 17; at most 64 rows go from one prefill block to one drafter block, and every drafter block receives exactly 64 from its own prefill block. The slots named in drafter block j are exactly its first counts[j] slots, grouped by k in that order. counts[j] is the number of prefill rows that name a slot of block j; some block is full. `fr_ids`: distinct ids.
All inputs are finite; a program needn't handle non-finite values.
Results may differ from a plain program's by a relative error of at most 0.0041.
Values may be sent and summed in bfloat16 or wider, within the bound.
A program may use at most 64 MiB of HBM per device.

v0:
```python
import jax
import jax.numpy as jnp
from jax import lax
from jax.sharding import PartitionSpec as P

loss_scale = 16.0


def encode(values):
    return jnp.stack([values // 128, values % 128], axis=1).astype(jnp.float32).astype(jnp.bfloat16)


def decode(code):
    widened = code.astype(jnp.float32)
    return (widened[:, 0] * 128.0 + widened[:, 1]).astype(jnp.int32)


def per_device(teacher_rows, drafter_rows, head, fr_ids, targets, dest_index, counts):
    row_count = teacher_rows.shape[0]
    tok_index = lax.axis_index("tok")
    first_slot = tok_index * row_count
    slot_ids = jnp.arange(row_count, dtype=jnp.int32)
    code = encode(dest_index + 1)
    rows_piece = lax.all_gather(teacher_rows, "tok", axis=0, tiled=True)
    code_piece = lax.all_gather(code, "tok", axis=0, tiled=True)
    wanted = decode(code_piece) - 1 - first_slot
    select = (slot_ids[:, None] == wanted[None, :]).astype(jnp.bfloat16)
    moved = jnp.dot(select, rows_piece, preferred_element_type=jnp.float32).astype(jnp.bfloat16)
    teacher_full, drafter_full = (
        lax.all_gather(moved, "voc", axis=1, tiled=True),
        lax.all_gather(drafter_rows, "voc", axis=1, tiled=True),
    )
    teach_logit = jnp.dot(teacher_full, head, preferred_element_type=jnp.float32)
    draft_logit = jnp.dot(drafter_full, head, preferred_element_type=jnp.float32)
    hit_table = (targets[:, None] == fr_ids[None, :]).astype(jnp.float32)
    local_hits = jnp.sum(hit_table, axis=1)
    local_target = jnp.sum(hit_table * draft_logit, axis=1)
    teach_max, draft_max = lax.pmax(
        (jnp.max(teach_logit, axis=1), jnp.max(draft_logit, axis=1)), "voc"
    )
    teach_exp = jnp.exp(teach_logit - teach_max[:, None])
    draft_exp = jnp.exp(draft_logit - draft_max[:, None])
    teach_total, draft_total, cross, target_logit, hits = lax.psum(
        (
            jnp.sum(teach_exp, axis=1),
            jnp.sum(draft_exp, axis=1),
            jnp.sum(teach_exp * (teach_logit - draft_logit), axis=1),
            local_target,
            local_hits,
        ),
        "voc",
    )
    valid = (slot_ids < counts[tok_index]).astype(jnp.float32)
    teach_lse = teach_max + jnp.log(teach_total)
    draft_lse = draft_max + jnp.log(draft_total)
    row_loss = valid * (
        cross / teach_total - teach_lse + draft_lse + hits * (draft_lse - target_logit)
    )
    teach_prob = teach_exp / teach_total[:, None]
    draft_prob = draft_exp / draft_total[:, None]
    grad_logit = (
        valid[:, None] * ((1.0 + hits)[:, None] * draft_prob - teach_prob - hit_table)
    ).astype(jnp.bfloat16)
    summed = lax.psum_scatter(
        lax.dot_general(
            head, grad_logit, (((1,), (1,)), ((), ())), preferred_element_type=jnp.float32
        ),
        "voc",
        scatter_dimension=0,
        tiled=True,
    )
    drafter_grad = (loss_scale * summed).T.astype(jnp.bfloat16)
    return (row_loss, drafter_grad)


def solution(mesh):
    return jax.shard_map(
        per_device,
        mesh=mesh,
        in_specs=(
            P("tok", "voc"),
            P("tok", "voc"),
            P(None, "voc"),
            P("voc"),
            P("tok"),
            P("tok"),
            P(),
        ),
        out_specs=(P("tok"), P("tok", "voc")),
        check_vma=False,
    )
```

profile of v0, /device:TPU:8, one launch (start us, length us, event | category | flops | bytes accessed | tf_op | source)
XLA Modules:
  0.0 239.7 jit_solution(6944104512413968319)
XLA Ops:
  7.2 0.0 all-gather.4.cloned.1.call-start
  7.2 0.7 all-gather.4.cloned.1.call-update
  7.9 0.0 all-gather.8.cloned.1.call-start
  7.9 0.7 all-gather.8.cloned.1.call-update
  8.6 0.0 all-gather.6.cloned.1.call-start
  8.7 0.7 and_select_fusion.1
  9.4 45.7 %all_gather.12 = bf16[8192,2]{0,1:T(2,128)(2,1)S(1)} all-gather(bf16[256,2]{0,1:T(2,128)(2,1)S(1)} %fusion.21), channel_id=1, replica_groups=mesh['tok'=32,'voc'=8] {'tok'}, dimensions={0}, use_global_device_ids=true | all-gather | bytes 33792 | tf_op jit(solution)/shard_map/all_gather | solution.py:25
  55.1 0.1 fusion.20
  55.2 38.8 %all-gather.4.cloned.1.call-done = bf16[8192,256]{1,0:T(8,128)(2,1)} async-done(((bf16[256,256]{1,0:T(8,128)(2,1)}), bf16[8192,256]{1,0:T(8,128)(2,1)}) %all-gather.4.cloned.1.call-update) | async-done | bytes 4194320 | tf_op jit(solution)/shard_map/all_gather | solution.py:24
  94.0 0.0 copy-start.2
  94.0 4.1 %fusion.7 = bf16[256,256]{1,0:T(8,128)(2,1)} fusion(bf16[8192,256]{1,0:T(8,128)(2,1)} %all-gather.4.cloned.1.call-done, s32[8192]{0:T(1024)S(1)} %bitcast.14), kind=kOutput, calls=%fused_computation.15 | convolution fusion | flops 1075904512 | bytes 4358144 | tf_op jit(solution)/shard_map/dot_general | solution.py:28
  98.2 0.0 all-gather.6.cloned.1.call-update
  98.2 0.0 reduce-scatter.2.cloned.1.call-start
  98.2 0.0 copy-done.2
  98.2 0.6 dynamic_slice.3
  98.8 0.5 fusion.22
  99.4 21.0 %all-gather.8.cloned.1.call-done = bf16[256,2048]{1,0:T(8,128)(2,1)} async-done(((bf16[256,256]{1,0:T(8,128)(2,1)}), bf16[256,2048]{1,0:T(8,128)(2,1)}) %all-gather.8.cloned.1.call-update) | async-done | bytes 1048592 | tf_op jit(solution)/shard_map/all_gather | solution.py:31
  120.3 6.1 %fusion.24 = (f32[256]{0:T(256)S(1)}, f32[256,2048]{1,0:T(8,128)S(1)}) fusion(bf16[256,2048]{1,0:T(8,128)(2,1)} %all-gather.8.cloned.1.call-done, bf16[2048,2048]{1,0:T(8,128)(2,1)} %param.9), kind=kOutput, calls=%fused_computation.45 | convolution fusion | flops 2148007680 | bytes 11535360 | tf_op jit(solution)/shard_map/dot_general | solution.py:34
  126.4 0.0 copy-start
  126.5 0.0 copy-start.1
  126.5 23.2 %all-gather.6.cloned.1.call-done = bf16[256,2048]{1,0:T(8,128)(2,1)} async-done(((bf16[256,256]{1,0:T(8,128)(2,1)}), bf16[256,2048]{1,0:T(8,128)(2,1)}) %all-gather.6.cloned.1.call-update) | async-done | bytes 1048592 | tf_op jit(solution)/shard_map/all_gather | solution.py:30
  149.7 7.4 %fusion.23 = (f32[256]{0:T(256)S(1)}, f32[256,2048]{1,0:T(8,128)}) fusion(bf16[256,2048]{1,0:T(8,128)(2,1)} %all-gather.6.cloned.1.call-done, bf16[2048,2048]{1,0:T(8,128)(2,1)} %param.9), kind=kOutput, calls=%fused_computation.44 | convolution fusion | flops 2148007680 | bytes 11535360 | tf_op jit(solution)/shard_map/dot_general | solution.py:33
  157.1 14.3 %all-reduce.1 = (f32[256]{0:T(256)S(1)}, f32[256]{0:T(256)S(1)}) all-reduce(f32[256]{0:T(256)S(1)} %get-tuple-element.18, f32[256]{0:T(256)S(1)} %get-tuple-element.20), channel_id=1, replica_groups=mesh['tok'=32,'voc'=8] {'voc'}, use_global_device_ids=true, to_apply=%region_1.2 | all-reduce | flops 512 | bytes 4096 | tf_op jit(solution)/shard_map/pmax | solution.py:38
  171.4 0.0 copy-done
  171.4 0.0 copy-done.1
  171.4 3.0 %multiply_reduce_fusion = (f32[256]{0:T(256)S(1)}, f32[256]{0:T(256)S(1)}, f32[256]{0:T(256)S(1)}, f32[256]{0:T(256)S(1)}, f32[256]{0:T(256)S(1)}) fusion(f32[256,2048]{1,0:T(8,128)} %get-tuple-element.19, f32[256,2048]{1,0:T(8,128)S(1)} %get-tuple-element.21, f32[256]{0:T(256)S(1)} %get-tuple-element.12, s32[2048]{0:T(1024)S(1)} %copy-done, ...), kind=kLoop, calls=%fused_computation.11 | loop fusion | flops 6290176 | bytes 4210688 | tf_op jit(solution)/shard_map/reduce_sum | solution.py:47
  174.4 12.6 %all-reduce = (f32[256]{0:T(256)S(1)}, f32[256]{0:T(256)S(1)}, f32[256]{0:T(256)S(1)}, f32[256]{0:T(256)S(1)}, f32[256]{0:T(256)S(1)}) all-reduce(f32[256]{0:T(256)S(1)} %get-tuple-element.6, f32[256]{0:T(256)S(1)} %get-tuple-element.4, f32[256]{0:T(256)S(1)} %get-tuple-element.5, ...), channel_id=1, replica_groups=mesh['tok'=32,'voc'=8] {'voc'}, use_global_device_ids=true, to_apply=%region_11.12 | all-reduce | flops 1280 | bytes 10240 | tf_op jit(solution)/shard_map/psum | solution.py:43
  187.1 1.1 broadcast_add_fusion
  188.2 8.3 %convolution_bitcast_fusion = f32[2048,256]{0,1:T(8,128)} fusion(bf16[2048,2048]{1,0:T(8,128)(2,1)} %param.9, f32[256,2048]{1,0:T(8,128)} %get-tuple-element.19, f32[256,2048]{1,0:T(8,128)S(1)} %get-tuple-element.21, f32[256]{0:T(256)S(1)} %get-tuple-element.10, f32[256]{0:T(256)S(1)} %get-tuple-element.9, f32[256]{0:T(256)S(1)} %get-tuple-element.14, ...), kind=kOutput, calls=%fused_computation.6 | convolution fusion | flops 2153250816 | bytes 14695424 | tf_op jit(solution)/shard_map/dot_general | solution.py:65
  196.4 0.0 reduce-scatter.2.cloned.1.call-update
  196.5 35.1 %reduce-scatter.2.cloned.1.call-done = f32[256,256]{0,1:T(8,128)} async-done(((f32[2048,256]{0,1:T(8,128)}), f32[256,256]{0,1:T(8,128)}) %reduce-scatter.2.cloned.1.call-update) | async-done | bytes 262160 | tf_op jit(solution)/shard_map/reduce_scatter | solution.py:64
  231.6 1.6 fusion.17
  (2 shorter events, 0.0 us)
Async XLA Ops:
  7.2 86.9 %all-gather.4.cloned.1.call-start = ((), (), s32[]{:S(2)}) async-start(), calls=%async_computation.1 | async-start | bytes 4325376 | tf_op jit(solution)/shard_map/all_gather | solution.py:24
  7.9 112.4 %all-gather.8.cloned.1.call-start = ((), (), s32[]{:S(2)}) async-start(), calls=%async_computation.3 | async-start | bytes 1179648 | tf_op jit(solution)/shard_map/all_gather | solution.py:31
  8.6 141.0 %all-gather.6.cloned.1.call-start = ((), (), s32[]{:S(2)}) async-start(), calls=%async_computation.2 | async-start | bytes 1179648 | tf_op jit(solution)/shard_map/all_gather | solution.py:30
  94.0 4.2 %copy-start.2 = (s32[32]{0:T(128)S(1)}, s32[32]{0:T(128)}, u32[]{:S(2)}) copy-start(s32[32]{0:T(128)} %param.13) | copy-start | bytes 388
  98.2 133.4 %reduce-scatter.2.cloned.1.call-start = ((), (), s32[]{:S(2)}) async-start(), calls=%async_computation.4 | async-start | bytes 2359296 | tf_op jit(solution)/shard_map/reduce_scatter | solution.py:64
  126.4 44.9 %copy-start = (s32[2048]{0:T(1024)S(1)}, s32[2048]{0:T(1024)}, u32[]{:S(2)}) copy-start(s32[2048]{0:T(1024)} %param.10) | copy-start | bytes 24580
  126.5 44.9 %copy-start.1 = (s32[256]{0:T(256)S(1)}, s32[256]{0:T(256)}, u32[]{:S(2)}) copy-start(s32[256]{0:T(256)} %param.11) | copy-start | bytes 3076
Sparse Core Ops, SparseCore 0:
  10.6 83.4 all-gather.3
  95.9 24.3 all-gather.7
  122.7 26.8 all-gather.5
  196.6 34.9 reduce-scatter.1
where the time goes:
time: 240 us
  waiting for transfers between devices  120 us (50%)
  blocking collectives  72.6 us (30%)
  matrix products  25.9 us (11%)
  between operations  13.8 us (6%)
  other arithmetic  7.13 us (3%)
    all_gather x1, blocking collectives, per_device(): code_piece = lax.all_gather(code, 'tok', axis=0, tiled=True)  45.7 us
    all_gather x1, waiting for transfers between devices, per_device(): rows_piece = lax.all_gather(teacher_rows, 'tok', axis=0, tiled=True)  38.8 us
    reduce_scatter x1, waiting for transfers between devices, per_device(): lax.psum_scatter(lax.dot_general(head, grad_logit, (((1,), (1,)), ((), ()...  35.1 us
    all_gather x1, waiting for transfers between devices, per_device(): lax.all_gather(moved, 'voc', axis=1, tiled=True)  23.2 us
    all_gather x1, waiting for transfers between devices, per_device(): lax.all_gather(drafter_rows, 'voc', axis=1, tiled=True)  21 us
    pmax x1, blocking collectives, per_device(): lax.pmax((jnp.max(teach_logit, axis=1), jnp.max(draft_logit, axis=1)), 'v...  14.3 us
    psum x1, blocking collectives, per_device(): lax.psum((jnp.sum(teach_exp, axis=1), jnp.sum(draft_exp, axis=1), jnp.sum...  12.6 us
    dot_general x1, matrix products, per_device(): lax.dot_general(head, grad_logit, (((1,), (1,)), ((), ())), preferred_ele...  8.27 us
  transfers between devices with their start and end apart: 4, of which 4 were waited for; matrix products, arithmetic and copies ran while one was open for 5% of the time, Pallas kernels for 0%

commit v1 on v0

--- a/solution.py
+++ b/solution.py
@@ -28,7 +28,9 @@
     moved = jnp.dot(select, rows_piece, preferred_element_type=jnp.float32).astype(jnp.bfloat16)
     teacher_full, drafter_full = (
         lax.all_gather(moved, "voc", axis=1, tiled=True),
-        lax.all_gather(drafter_rows, "voc", axis=1, tiled=True),
+        jnp.concatenate(
+            lax.all_to_all(jnp.stack([drafter_rows] * lax.axis_size("voc")), "voc", 0, 0), axis=1
+        ),
     )
     teach_logit = jnp.dot(teacher_full, head, preferred_element_type=jnp.float32)
     draft_logit = jnp.dot(drafter_full, head, preferred_element_type=jnp.float32)

time: 240 us -> 216 us (0.900)
  waiting for transfers between devices: 120 us -> 91.3 us
  starting transfers between devices: 0.16 us -> 4.38 us
    all_gather x1, waiting for transfers between devices: 23.2 us -> 0.02 us  [per_device(): lax.all_gather(moved, 'voc', axis=1, tiled=True)]
    all_gather x1 -> x0, waiting for transfers between devices: 21 us -> none  [per_device(): lax.all_gather(drafter_rows, 'voc', axis=1, tiled=True)]
    all_to_all x0 -> x1, waiting for transfers between devices: none -> 17.6 us  [per_device(): lax.all_to_all(jnp.stack([drafter_rows] * lax.axis_size('voc')), 'voc', 0...]
    all_to_all x0 -> x1, starting transfers between devices: none -> 4.26 us  [per_device(): lax.all_to_all(jnp.stack([drafter_rows] * lax.axis_size('voc')), 'voc', 0...]
  transfers between devices with their start and end apart: 4 -> 4, of which waited for: 4 -> 3; matrix products, arithmetic and copies ran while one was open for 5% -> 4% of each run, Pallas kernels for 0% -> 0%
where the time goes in v1:
time: 216 us; the launch traced here: 215 us
  waiting for transfers between devices  91.3 us (42%)
  blocking collectives  71.1 us (33%)
  matrix products  25.6 us (12%)
  between operations  13.8 us (6%)
  other arithmetic  7.13 us (3%)
  starting transfers between devices  4.38 us (2%)
    all_gather x1, blocking collectives, per_device(): code_piece = lax.all_gather(code, 'tok', axis=0, tiled=True)  45.7 us
    all_gather x1, waiting for transfers between devices, per_device(): rows_piece = lax.all_gather(teacher_rows, 'tok', axis=0, tiled=True)  39.6 us
    reduce_scatter x1, waiting for transfers between devices, per_device(): lax.psum_scatter(lax.dot_general(head, grad_logit, (((1,), (1,)), ((), ()...  33.4 us
    all_to_all x1, waiting for transfers between devices, per_device(): lax.all_to_all(jnp.stack([drafter_rows] * lax.axis_size('voc')), 'voc', 0...  17.6 us
    pmax x1, blocking collectives, per_device(): lax.pmax((jnp.max(teach_logit, axis=1), jnp.max(draft_logit, axis=1)), 'v...  12.8 us
    psum x1, blocking collectives, per_device(): lax.psum((jnp.sum(teach_exp, axis=1), jnp.sum(draft_exp, axis=1), jnp.sum...  12.6 us
    dot_general x1, matrix products, per_device(): lax.dot_general(head, grad_logit, (((1,), (1,)), ((), ())), preferred_ele...  8.28 us
    dot_general x1, matrix products, per_device(): jnp.dot(teacher_full, head, preferred_element_type=jnp.float32)  7.41 us
  transfers between devices with their start and end apart: 4, of which 3 were waited for; matrix products, arithmetic and copies ran while one was open for 4% of the time, Pallas kernels for 0%

profile of v1, /device:TPU:8, one launch (start us, length us, event | category | flops | bytes accessed | tf_op | source)
XLA Modules:
  0.0 215.2 jit_solution(14941050520527351264)
XLA Ops:
  7.2 0.0 all-gather.3.cloned.1.call-start
  7.2 0.7 all-gather.3.cloned.1.call-update
  7.9 0.0 all-gather.5.cloned.1.call-start
  7.9 0.7 and_select_fusion.1
  8.7 45.7 %all_gather.9 = bf16[8192,2]{0,1:T(2,128)(2,1)S(1)} all-gather(bf16[256,2]{0,1:T(2,128)(2,1)S(1)} %fusion.21), channel_id=1, replica_groups=mesh['tok'=32,'voc'=8] {'tok'}, dimensions={0}, use_global_device_ids=true | all-gather | bytes 33792 | tf_op jit(solution)/shard_map/all_gather | solution.py:25
  54.4 0.1 fusion.20
  54.4 39.6 %all-gather.3.cloned.1.call-done = bf16[8192,256]{1,0:T(8,128)(2,1)} async-done(((bf16[256,256]{1,0:T(8,128)(2,1)}), bf16[8192,256]{1,0:T(8,128)(2,1)}) %all-gather.3.cloned.1.call-update) | async-done | bytes 4194320 | tf_op jit(solution)/shard_map/all_gather | solution.py:24
  94.0 0.0 copy-start
  94.0 4.1 %fusion.7 = bf16[256,256]{1,0:T(8,128)(2,1)} fusion(bf16[8192,256]{1,0:T(8,128)(2,1)} %all-gather.3.cloned.1.call-done, s32[8192]{0:T(1024)S(1)} %bitcast.18), kind=kOutput, calls=%fused_computation.15 | convolution fusion | flops 1075904512 | bytes 4358144 | tf_op jit(solution)/shard_map/dot_general | solution.py:28
  98.2 0.0 copy-start.3
  98.2 0.0 all-gather.5.cloned.1.call-update
  98.2 0.0 copy-done
  98.2 0.1 copy.9
  98.3 1.1 stack.11
  99.4 4.3 %all-to-all-start = ((bf16[8,256,256]{1,2,0:T(8,128)(2,1)}), bf16[8,256,256]{1,2,0:T(8,128)(2,1)S(1)}, u32[]{:S(2)}, u32[]{:S(2)}) async-start(bf16[8,256,256]{1,2,0:T(8,128)(2,1)} %stack.11), calls=%async_computation | async-start | bytes 2097152 | tf_op jit(solution)/shard_map/all_to_all | solution.py:32
  103.6 0.0 reduce-scatter.2.cloned.1.call-start
  103.7 0.0 copy-done.3
  103.7 0.6 dynamic_slice.3
  104.2 0.5 fusion.22
  104.8 17.6 %all-to-all-done = bf16[8,256,256]{1,2,0:T(8,128)(2,1)S(1)} async-done(((bf16[8,256,256]{1,2,0:T(8,128)(2,1)}), bf16[8,256,256]{1,2,0:T(8,128)(2,1)S(1)}, u32[]{:S(2)}, u32[]{:S(2)}) %all-to-all-start) | async-done | bytes 1048608 | tf_op jit(solution)/shard_map/all_to_all | solution.py:32
  122.4 5.8 %fusion.24 = (f32[256]{0:T(256)S(1)}, f32[256,2048]{1,0:T(8,128)S(1)}) fusion(bf16[256,2048]{0,1:T(8,128)(2,1)S(1)} %bitcast.17, bf16[2048,2048]{1,0:T(8,128)(2,1)} %param.9), kind=kOutput, calls=%fused_computation.45 | convolution fusion | flops 2148007680 | bytes 11535360 | tf_op jit(solution)/shard_map/dot_general | solution.py:36
  128.2 0.0 copy-start.1
  128.2 0.0 copy-start.2
  128.2 0.0 all-gather.5.cloned.1.call-done
  128.3 7.4 %fusion.23 = (f32[256]{0:T(256)S(1)}, f32[256,2048]{1,0:T(8,128)}) fusion(bf16[256,2048]{1,0:T(8,128)(2,1)} %all-gather.5.cloned.1.call-done, bf16[2048,2048]{1,0:T(8,128)(2,1)} %param.9), kind=kOutput, calls=%fused_computation.44 | convolution fusion | flops 2148007680 | bytes 11535360 | tf_op jit(solution)/shard_map/dot_general | solution.py:35
  135.7 12.8 %all-reduce.1 = (f32[256]{0:T(256)S(1)}, f32[256]{0:T(256)S(1)}) all-reduce(f32[256]{0:T(256)S(1)} %get-tuple-element.18, f32[256]{0:T(256)S(1)} %get-tuple-element.20), channel_id=1, replica_groups=mesh['tok'=32,'voc'=8] {'voc'}, use_global_device_ids=true, to_apply=%region_1.2 | all-reduce | flops 512 | bytes 4096 | tf_op jit(solution)/shard_map/pmax | solution.py:40
  148.5 0.0 copy-done.1
  148.5 0.0 copy-done.2
  148.5 3.0 %multiply_reduce_fusion = (f32[256]{0:T(256)S(1)}, f32[256]{0:T(256)S(1)}, f32[256]{0:T(256)S(1)}, f32[256]{0:T(256)S(1)}, f32[256]{0:T(256)S(1)}) fusion(f32[256,2048]{1,0:T(8,128)} %get-tuple-element.19, f32[256,2048]{1,0:T(8,128)S(1)} %get-tuple-element.21, f32[256]{0:T(256)S(1)} %get-tuple-element.12, s32[2048]{0:T(1024)S(1)} %copy-done.1, ...), kind=kLoop, calls=%fused_computation.11 | loop fusion | flops 6290176 | bytes 4210688 | tf_op jit(solution)/shard_map/reduce_sum | solution.py:49
  151.6 12.6 %all-reduce = (f32[256]{0:T(256)S(1)}, f32[256]{0:T(256)S(1)}, f32[256]{0:T(256)S(1)}, f32[256]{0:T(256)S(1)}, f32[256]{0:T(256)S(1)}) all-reduce(f32[256]{0:T(256)S(1)} %get-tuple-element.6, f32[256]{0:T(256)S(1)} %get-tuple-element.4, f32[256]{0:T(256)S(1)} %get-tuple-element.5, ...), channel_id=1, replica_groups=mesh['tok'=32,'voc'=8] {'voc'}, use_global_device_ids=true, to_apply=%region_11.12 | all-reduce | flops 1280 | bytes 10240 | tf_op jit(solution)/shard_map/psum | solution.py:45
  164.2 1.1 broadcast_add_fusion
  165.3 8.3 %convolution_bitcast_fusion = f32[2048,256]{0,1:T(8,128)} fusion(bf16[2048,2048]{1,0:T(8,128)(2,1)} %param.9, f32[256,2048]{1,0:T(8,128)} %get-tuple-element.19, f32[256,2048]{1,0:T(8,128)S(1)} %get-tuple-element.21, f32[256]{0:T(256)S(1)} %get-tuple-element.10, f32[256]{0:T(256)S(1)} %get-tuple-element.9, f32[256]{0:T(256)S(1)} %get-tuple-element.14, ...), kind=kOutput, calls=%fused_computation.6 | convolution fusion | flops 2153250816 | bytes 14695424 | tf_op jit(solution)/shard_map/dot_general | solution.py:67
  173.6 0.0 reduce-scatter.2.cloned.1.call-update
  173.6 33.4 %reduce-scatter.2.cloned.1.call-done = f32[256,256]{0,1:T(8,128)} async-done(((f32[2048,256]{0,1:T(8,128)}), f32[256,256]{0,1:T(8,128)}) %reduce-scatter.2.cloned.1.call-update) | async-done | bytes 262160 | tf_op jit(solution)/shard_map/reduce_scatter | solution.py:66
  207.0 1.6 fusion.17
  (2 shorter events, 0.0 us)
Async XLA Ops:
  7.2 86.9 %all-gather.3.cloned.1.call-start = ((), (), s32[]{:S(2)}) async-start(), calls=%async_computation.2 | async-start | bytes 4325376 | tf_op jit(solution)/shard_map/all_gather | solution.py:24
  7.9 120.4 %all-gather.5.cloned.1.call-start = ((), (), s32[]{:S(2)}) async-start(), calls=%async_computation.3 | async-start | bytes 1179648 | tf_op jit(solution)/shard_map/all_gather | solution.py:30
  94.0 4.2 %copy-start = (bf16[256,256]{1,0:T(8,128)(2,1)S(1)}, bf16[256,256]{1,0:T(8,128)(2,1)}, u32[]{:S(2)}) copy-start(bf16[256,256]{1,0:T(8,128)(2,1)} %param.8) | copy-start | bytes 393220
  98.2 5.5 %copy-start.3 = (s32[32]{0:T(128)S(1)}, s32[32]{0:T(128)}, u32[]{:S(2)}) copy-start(s32[32]{0:T(128)} %param.13) | copy-start | bytes 388
  99.4 23.0 %all-to-all-start = ((bf16[8,256,256]{1,2,0:T(8,128)(2,1)}), bf16[8,256,256]{1,2,0:T(8,128)(2,1)S(1)}, u32[]{:S(2)}, u32[]{:S(2)}) async-start(bf16[8,256,256]{1,2,0:T(8,128)(2,1)} %stack.11), calls=%async_computation | async-start | bytes 2097152 | tf_op jit(solution)/shard_map/all_to_all | solution.py:32
  103.6 103.4 %reduce-scatter.2.cloned.1.call-start = ((), (), s32[]{:S(2)}) async-start(), calls=%async_computation.4 | async-start | bytes 2359296 | tf_op jit(solution)/shard_map/reduce_scatter | solution.py:66
  128.2 20.3 %copy-start.1 = (s32[2048]{0:T(1024)S(1)}, s32[2048]{0:T(1024)}, u32[]{:S(2)}) copy-start(s32[2048]{0:T(1024)} %param.10) | copy-start | bytes 24580
  128.2 20.3 %copy-start.2 = (s32[256]{0:T(256)S(1)}, s32[256]{0:T(256)}, u32[]{:S(2)}) copy-start(s32[256]{0:T(256)} %param.11) | copy-start | bytes 3076
Sparse Core Ops, SparseCore 0:
  10.6 83.4 all-gather.2
  98.3 27.6 all-gather.4
  173.8 33.2 reduce-scatter.1
